TPU v7x, 256 devices: a whole 4x4x8 slice. The times are simulated.
256 devices in a mesh: dp: 32 (over z_hi, y, core), tensor: 8 (over x, z_lo).
Axes of the slice: x: 4, y: 4, z: 8 (z_hi: 4, z_lo: 2; z = z_hi * 2 + z_lo), core: 2. Of those that a mesh axis runs over, the one named last changes fastest.
Arguments:
- hidden: bfloat16 [32, 1024, 28672], P('dp', None, 'tensor'), may hold values from -6 to 6
- grad_out: bfloat16 [32, 1024, 8192], P('dp', None, 'tensor'), may hold values from -30 to 30
- proj_in: bfloat16 [64, 28672], P(None, 'tensor'), may hold values from -0.03125 to 0.03125
- proj_out: bfloat16 [64, 8192], P(None, 'tensor'), may hold values from -0.0625 to 0.0625
Outputs:
- covariance: float32 [4096, 4096], P('dp', 'tensor')
All inputs are finite; a program needn't handle non-finite values.
Results may differ from a plain program's by a relative error of at most 0.0003.
Values sent between devices are 32-bit elements; how exact they have to be, the bound alone decides.
No kernel may reach another device: no remote copies, remote signals or barrier semaphores. Data moves between devices by JAX's collectives and lax.ppermute only.
A program may use at most 64 MiB of HBM per device.

v0:
```python
import math
import jax
import jax.numpy as jnp
from jax import lax
from jax.sharding import PartitionSpec as P


def outer_sum(panels, width):
    left_side = panels[:, :, :width]
    right_side = panels[:, :, width:]
    return jnp.einsum(
        "sta,stb->sab",
        left_side,
        right_side,
        precision=lax.Precision.HIGHEST,
        preferred_element_type=jnp.float32,
    )


def shards(hidden, grad_out, proj_in, proj_out):
    seqs_here = hidden.shape[0]
    length = hidden.shape[1]
    width = proj_in.shape[0]
    inv_root = 1.0 / math.sqrt(length)
    in_panel = jnp.einsum("stf,af->sta", hidden, proj_in, preferred_element_type=jnp.float32)
    out_panel = jnp.einsum("ste,be->stb", grad_out, proj_out, preferred_element_type=jnp.float32)
    panels = jnp.concatenate([in_panel, out_panel], axis=2)
    summed = lax.psum(panels, "tensor")
    seq_outer = outer_sum(summed, width)
    flat_grads = (seq_outer * inv_root).reshape(seqs_here, width * width)
    total_len = width * width
    col_count = total_len // lax.axis_size("tensor")
    row_count = total_len // lax.axis_size("dp")
    col_begin = lax.axis_index("tensor") * col_count
    row_begin = lax.axis_index("dp") * row_count
    all_seqs = seqs_here * lax.axis_size("dp")
    gathered = lax.all_gather(flat_grads, "dp", axis=0, tiled=True)
    row_part = lax.dynamic_slice_in_dim(gathered, row_begin, row_count, 1)
    col_block = lax.dynamic_slice_in_dim(gathered, col_begin, col_count, 1)
    raw_block = jnp.dot(
        row_part.T, col_block, precision=lax.Precision.HIGHEST, preferred_element_type=jnp.float32
    )
    trace_total = jnp.sum(gathered * gathered)
    damping = 0.5 * trace_total / (all_seqs * total_len)
    row_ids = row_begin + lax.broadcasted_iota(jnp.int32, (row_count, col_count), 0)
    col_ids = col_begin + lax.broadcasted_iota(jnp.int32, (row_count, col_count), 1)
    diagonal = jnp.where(row_ids == col_ids, damping, jnp.float32(0.0))
    return raw_block / all_seqs + diagonal


def solution(mesh):
    placed = (
        P("dp", None, "tensor"),
        P("dp", None, "tensor"),
        P(None, "tensor"),
        P(None, "tensor"),
    )
    return jax.shard_map(
        shards, mesh=mesh, in_specs=placed, out_specs=P("dp", "tensor"), check_vma=False
    )
```

profile of v0, /device:TPU:1, one launch (start us, length us, event | category | flops | bytes accessed | tf_op | source)
XLA Modules:
  0.0 158.4 jit_solution(9999071487780403758)
XLA Ops:
  6.5 0.0 copy-start
  6.5 0.0 all-reduce.2.cloned.1.call-start
  6.5 1.6 %copy-done = bf16[1,1024,1024]{2,1,0:T(8,128)(2,1)S(1)} copy-done((bf16[1,1024,1024]{2,1,0:T(8,128)(2,1)S(1)}, bf16[1,1024,1024]{2,1,0:T(8,128)(2,1)}, u32[]{:S(2)}) %copy-start) | copy-done | bytes 2097176
  8.1 1.7 %fusion.4 = f32[1,1024,64]{1,2,0:T(8,128)S(1)} fusion(bf16[64,1024]{1,0:T(8,128)(2,1)} %param.7, bf16[1,1024,1024]{2,1,0:T(8,128)(2,1)S(1)} %copy-done), kind=kOutput, calls=%fused_computation.4 | convolution fusion | flops 134217728 | bytes 2490368 | tf_op jit(solution)/shard_map/ste,be->stb/dot_general | solution.py:26
  9.8 5.4 %fusion.8 = f32[1,1024,64]{1,2,0:T(8,128)S(1)} fusion(bf16[64,3584]{1,0:T(8,128)(2,1)} %param.6, bf16[1,1024,3584]{2,1,0:T(8,128)(2,1)} %param.4), kind=kOutput, calls=%fused_computation.7 | convolution fusion | flops 469762048 | bytes 8060928 | tf_op jit(solution)/shard_map/stf,af->sta/dot_general | solution.py:25
  15.2 0.9 pad_maximum_fusion
  16.1 0.0 all-reduce.2.cloned.1.call-update
  16.1 79.5 %all-reduce.2.cloned.1.call-done = f32[1,1024,128]{1,2,0:T(8,128)} async-done(((f32[1,1024,128]{1,2,0:T(8,128)}), f32[1,1024,128]{1,2,0:T(8,128)}) %all-reduce.2.cloned.1.call-update) | async-done | bytes 524304 | tf_op jit(solution)/shard_map/psum | solution.py:28
  95.6 1.4 convolution_multiply_fusion.1
  97.0 0.1 reshape.25
  97.1 51.0 %all-gather = f32[32,1,4096]{2,1,0:T(1,128)S(1)} all-gather(f32[1,1,4096]{2,1,0:T(1,128)S(1)} %reshape.25), channel_id=1, replica_groups=mesh['dp'=32,'tensor'=8] {'dp'}, dimensions={0}, use_global_device_ids=true | all-gather | bytes 540672 | tf_op jit(solution)/shard_map/all_gather | solution.py:37
  148.1 1.7 %multiply_reduce_fusion = f32[]{:T(128)} fusion(f32[32,1,4096]{2,1,0:T(1,128)S(1)} %all-gather), kind=kLoop, calls=%fused_computation.10 | loop fusion | flops 262143 | bytes 524292 | tf_op jit(solution)/shard_map/reduce_sum | solution.py:43
  150.5 1.1 fusion.7
  (4 shorter events, 0.1 us)
Async XLA Ops:
  6.5 1.6 %copy-start = (bf16[1,1024,1024]{2,1,0:T(8,128)(2,1)S(1)}, bf16[1,1024,1024]{2,1,0:T(8,128)(2,1)}, u32[]{:S(2)}) copy-start(bf16[1,1024,1024]{2,1,0:T(8,128)(2,1)} %param.5) | copy-start | bytes 6291460
  6.5 89.1 %all-reduce.2.cloned.1.call-start = ((), (), s32[]{:S(2)}) async-start(), calls=%async_computation | async-start | bytes 1048576 | tf_op jit(solution)/shard_map/psum | solution.py:28
Sparse Core Ops, SparseCore 0:
  16.2 79.3 all-reduce.1
where the time goes:
time: 159 us; the launch traced here: 158 us
  waiting for transfers between devices  79.5 us (50%)
  blocking collectives  51 us (32%)
  between operations  14.1 us (9%)
  matrix products  9.61 us (6%)
  other arithmetic  2.55 us (2%)
  local copies, waits for them, and re-layouts  1.72 us (1%)
    psum x1, waiting for transfers between devices, shards(): summed = lax.psum(panels, 'tensor')  79.5 us
    all_gather x1, blocking collectives, shards(): gathered = lax.all_gather(flat_grads, 'dp', axis=0, tiled=True)  51 us
    dot_general x1, matrix products, shards(): jnp.einsum('stf,af->sta', hidden, proj_in, preferred_element_type=jnp.flo...  5.43 us
  transfers between devices with their start and end apart: 1, of which 1 were waited for; matrix products, arithmetic and copies ran while one was open for 0% of the time, Pallas kernels for 0%

commit v1 on v0

--- a/solution.py
+++ b/solution.py
@@ -25,7 +25,7 @@
     in_panel = jnp.einsum("stf,af->sta", hidden, proj_in, preferred_element_type=jnp.float32)
     out_panel = jnp.einsum("ste,be->stb", grad_out, proj_out, preferred_element_type=jnp.float32)
     panels = jnp.concatenate([in_panel, out_panel], axis=2)
-    summed = lax.psum(panels, "tensor")
+    summed = jnp.sum(lax.all_gather(panels, "tensor"), axis=0)
     seq_outer = outer_sum(summed, width)
     flat_grads = (seq_outer * inv_root).reshape(seqs_here, width * width)
     total_len = width * width

time: 159 us -> 174 us (1.094)
  waiting for transfers between devices: 79.5 us -> 97 us
  blocking collectives: 51 us -> 46.6 us
    all_gather x0 -> x1, waiting for transfers between devices: none -> 97 us  [shards(): summed = jnp.sum(lax.all_gather(panels, 'tensor'), axis=0)]
    psum x1 -> x0, waiting for transfers between devices: 79.5 us -> none  [shards(): summed = lax.psum(panels, 'tensor')]
    all_gather x1, blocking collectives: 51 us -> 46.6 us  [shards(): gathered = lax.all_gather(flat_grads, 'dp', axis=0, tiled=True)]
    reduce_sum x0 -> x1, other arithmetic: none -> 2.45 us  [shards(): summed = jnp.sum(lax.all_gather(panels, 'tensor'), axis=0)]
where the time goes in v1:
time: 174 us; the launch traced here: 173 us
  waiting for transfers between devices  97 us (56%)
  blocking collectives  46.6 us (27%)
  between operations  14.1 us (8%)
  matrix products  8.58 us (5%)
  other arithmetic  4.18 us (2%)
  local copies, waits for them, and re-layouts  2.91 us (2%)
    all_gather x1, waiting for transfers between devices, shards(): summed = jnp.sum(lax.all_gather(panels, 'tensor'), axis=0)  97 us
    all_gather x1, blocking collectives, shards(): gathered = lax.all_gather(flat_grads, 'dp', axis=0, tiled=True)  46.6 us
    dot_general x1, matrix products, shards(): jnp.einsum('stf,af->sta', hidden, proj_in, preferred_element_type=jnp.flo...  5.43 us
  transfers between devices with their start and end apart: 1, of which 1 were waited for; matrix products, arithmetic and copies ran while one was open for 0% of the time, Pallas kernels for 0%

profile of v1, /device:TPU:1, one launch (start us, length us, event | category | flops | bytes accessed | tf_op | source)
XLA Modules:
  0.0 173.4 jit_solution(16798493711488814419)
XLA Ops:
  6.5 0.0 copy-start
  6.5 0.0 all-gather.4.cloned.1.call-start
  6.5 1.6 copy-done
  8.1 1.7 fusion.4
  9.8 5.4 %fusion.8 = f32[1,1024,64]{1,2,0:T(8,128)S(1)} fusion(bf16[64,3584]{1,0:T(8,128)(2,1)} %param.6, bf16[1,1024,3584]{2,1,0:T(8,128)(2,1)} %param.4), kind=kOutput, calls=%fused_computation.7 | convolution fusion | flops 469762048 | bytes 8060928 | tf_op jit(solution)/shard_map/stf,af->sta/dot_general | solution.py:25
  15.3 1.0 copy.5
  16.3 0.0 all-gather.4.cloned.1.call-update
  16.3 97.0 %all-gather.4.cloned.1.call-done = f32[8,1024,128]{2,1,0:T(8,128)} async-done(((f32[1,1024,128]{2,1,0:T(8,128)}), f32[8,1024,128]{2,1,0:T(8,128)}) %all-gather.4.cloned.1.call-update) | async-done | bytes 4194320 | tf_op jit(solution)/shard_map/all_gather | solution.py:28
  113.3 2.4 %reduce.1 = f32[1024,128]{1,0:T(8,128)S(1)} reduce(f32[8,1024,128]{2,1,0:T(8,128)} %all-gather.4.cloned.1.call-done, f32[]{:T(128)} %constant.10.clone.1), dimensions={0}, to_apply=%region_0.0 | reduce | flops 917504 | bytes 4718596 | tf_op jit(solution)/shard_map/reduce_sum | solution.py:28
  115.8 0.2 copy.8
  116.0 0.4 convolution_multiply_fusion.1
  116.3 0.1 reshape.28
  116.4 46.6 %all-gather.1 = f32[32,1,4096]{2,1,0:T(1,128)S(1)} all-gather(f32[1,1,4096]{2,1,0:T(1,128)S(1)} %reshape.28), channel_id=1, replica_groups=mesh['dp'=32,'tensor'=8] {'dp'}, dimensions={0}, use_global_device_ids=true | all-gather | bytes 540672 | tf_op jit(solution)/shard_map/all_gather | solution.py:37
  163.0 1.7 multiply_reduce_fusion
  165.4 1.1 fusion.7
  (5 shorter events, 0.1 us)
Async XLA Ops:
  6.5 1.6 copy-start
  6.5 106.8 %all-gather.4.cloned.1.call-start = ((), (), s32[]{:S(2)}) async-start(), calls=%async_computation | async-start | bytes 4718592 | tf_op jit(solution)/shard_map/all_gather | solution.py:28
Sparse Core Ops, SparseCore 0:
  16.4 96.8 all-gather.3

commit v2 on v0

--- a/solution.py
+++ b/solution.py
@@ -34,7 +34,9 @@
     col_begin = lax.axis_index("tensor") * col_count
     row_begin = lax.axis_index("dp") * row_count
     all_seqs = seqs_here * lax.axis_size("dp")
-    gathered = lax.all_gather(flat_grads, "dp", axis=0, tiled=True)
+    gathered = jnp.concatenate(
+        lax.all_to_all(jnp.stack([flat_grads] * lax.axis_size("dp")), "dp", 0, 0), axis=0
+    )
     row_part = lax.dynamic_slice_in_dim(gathered, row_begin, row_count, 1)
     col_block = lax.dynamic_slice_in_dim(gathered, col_begin, col_count, 1)
     raw_block = jnp.dot(

time: 159 us -> 140 us (0.88)
  blocking collectives: 51 us -> 0 us
  waiting for transfers between devices: 79.5 us -> 97.3 us
  starting transfers between devices: 0.01 us -> 14.1 us
    all_gather x1 -> x0, blocking collectives: 51 us -> none  [shards(): gathered = lax.all_gather(flat_grads, 'dp', axis=0, tiled=True)]
    all_to_all x0 -> x1, waiting for transfers between devices: none -> 17.8 us  [shards(): lax.all_to_all(jnp.stack([flat_grads] * lax.axis_size('dp')), 'dp', 0, 0)]
    all_to_all x0 -> x1, starting transfers between devices: none -> 14.1 us  [shards(): lax.all_to_all(jnp.stack([flat_grads] * lax.axis_size('dp')), 'dp', 0, 0)]
  transfers between devices with their start and end apart: 1 -> 2, of which waited for: 1 -> 2; matrix products, arithmetic and copies ran while one was open for 0% -> 0% of each run, Pallas kernels for 0% -> 0%
where the time goes in v2:
time: 140 us
  waiting for transfers between devices  97.3 us (70%)
  starting transfers between devices  14.1 us (10%)
  between operations  14.1 us (10%)
  matrix products  9.61 us (7%)
  local copies, waits for them, and re-layouts  2.97 us (2%)
  other arithmetic  1.74 us (1%)
    psum x1, waiting for transfers between devices, shards(): summed = lax.psum(panels, 'tensor')  79.5 us
    all_to_all x1, waiting for transfers between devices, shards(): lax.all_to_all(jnp.stack([flat_grads] * lax.axis_size('dp')), 'dp', 0, 0)  17.8 us
    all_to_all x1, starting transfers between devices, shards(): lax.all_to_all(jnp.stack([flat_grads] * lax.axis_size('dp')), 'dp', 0, 0)  14.1 us
    dot_general x1, matrix products, shards(): jnp.einsum('stf,af->sta', hidden, proj_in, preferred_element_type=jnp.flo...  5.43 us
  transfers between devices with their start and end apart: 2, of which 2 were waited for; matrix products, arithmetic and copies ran while one was open for 0% of the time, Pallas kernels for 0%

profile of v2, /device:TPU:1, one launch (start us, length us, event | category | flops | bytes accessed | tf_op | source)
XLA Modules:
  0.0 139.8 jit_solution(12635366835619158650)
XLA Ops:
  6.5 0.0 copy-start
  6.5 0.0 all-reduce.2.cloned.1.call-start
  6.5 1.6 %copy-done = bf16[1,1024,1024]{2,1,0:T(8,128)(2,1)S(1)} copy-done((bf16[1,1024,1024]{2,1,0:T(8,128)(2,1)S(1)}, bf16[1,1024,1024]{2,1,0:T(8,128)(2,1)}, u32[]{:S(2)}) %copy-start) | copy-done | bytes 2097176
  8.1 1.7 %fusion.4 = f32[1,1024,64]{1,2,0:T(8,128)S(1)} fusion(bf16[64,1024]{1,0:T(8,128)(2,1)} %param.7, bf16[1,1024,1024]{2,1,0:T(8,128)(2,1)S(1)} %copy-done), kind=kOutput, calls=%fused_computation.4 | convolution fusion | flops 134217728 | bytes 2490368 | tf_op jit(solution)/shard_map/ste,be->stb/dot_general | solution.py:26
  9.8 5.4 %fusion.8 = f32[1,1024,64]{1,2,0:T(8,128)S(1)} fusion(bf16[64,3584]{1,0:T(8,128)(2,1)} %param.6, bf16[1,1024,3584]{2,1,0:T(8,128)(2,1)} %param.4), kind=kOutput, calls=%fused_computation.7 | convolution fusion | flops 469762048 | bytes 8060928 | tf_op jit(solution)/shard_map/stf,af->sta/dot_general | solution.py:25
  15.2 0.9 pad_maximum_fusion
  16.1 0.0 all-reduce.2.cloned.1.call-update
  16.1 79.5 %all-reduce.2.cloned.1.call-done = f32[1,1024,128]{1,2,0:T(8,128)} async-done(((f32[1,1024,128]{1,2,0:T(8,128)}), f32[1,1024,128]{1,2,0:T(8,128)}) %all-reduce.2.cloned.1.call-update) | async-done | bytes 524304 | tf_op jit(solution)/shard_map/psum | solution.py:28
  95.6 1.4 convolution_multiply_fusion.1
  97.0 0.1 stack_reshape.2
  97.1 1.3 stack.3
  98.4 14.1 %all-to-all-start = ((f32[32,1,4096]{2,1,0:T(1,128)}), f32[32,1,4096]{2,1,0:T(1,128)S(1)}, u32[]{:S(2)}, u32[]{:S(2)}) async-start(f32[32,1,4096]{2,1,0:T(1,128)} %stack.3), calls=%async_computation | async-start | bytes 1048576 | tf_op jit(solution)/shard_map/all_to_all | solution.py:38
  112.5 17.8 %all-to-all-done = f32[32,1,4096]{2,1,0:T(1,128)S(1)} async-done(((f32[32,1,4096]{2,1,0:T(1,128)}), f32[32,1,4096]{2,1,0:T(1,128)S(1)}, u32[]{:S(2)}, u32[]{:S(2)}) %all-to-all-start) | async-done | bytes 524320 | tf_op jit(solution)/shard_map/all_to_all | solution.py:38
  130.2 0.9 fusion.11
  131.8 1.1 fusion.7
  (4 shorter events, 0.1 us)
Async XLA Ops:
  6.5 1.6 %copy-start = (bf16[1,1024,1024]{2,1,0:T(8,128)(2,1)S(1)}, bf16[1,1024,1024]{2,1,0:T(8,128)(2,1)}, u32[]{:S(2)}) copy-start(bf16[1,1024,1024]{2,1,0:T(8,128)(2,1)} %param.5) | copy-start | bytes 6291460
  6.5 89.1 %all-reduce.2.cloned.1.call-start = ((), (), s32[]{:S(2)}) async-start(), calls=%async_computation.1 | async-start | bytes 1048576 | tf_op jit(solution)/shard_map/psum | solution.py:28
  98.4 31.9 %all-to-all-start = ((f32[32,1,4096]{2,1,0:T(1,128)}), f32[32,1,4096]{2,1,0:T(1,128)S(1)}, u32[]{:S(2)}, u32[]{:S(2)}) async-start(f32[32,1,4096]{2,1,0:T(1,128)} %stack.3), calls=%async_computation | async-start | bytes 1048576 | tf_op jit(solution)/shard_map/all_to_all | solution.py:38
Sparse Core Ops, SparseCore 0:
  16.2 79.3 all-reduce.1
